TPU v7x, 32 devices: a whole 2x2x4 slice. The times are simulated.
32 devices in a mesh: dp: 8 (over y, x, core), expert: 4 (over z).
Axes of the slice: x: 2, y: 2, z: 4, core: 2. Of those that a mesh axis runs over, the one named last changes fastest.
Arguments:
- tokens: bfloat16 [2, 8192, 512], P(None, ('dp', 'expert')), may hold values from -6 to 6
- image_ids: int32 [2, 8192], P(None, ('dp', 'expert')), may hold values from 0 to 41, never falling along the last dimension, each value on 1 to 197 neighbouring positions
- routes: int32 [2, 8192, 2], P(None, ('dp', 'expert')), may hold values from 0 to 7, all different within a row; in each aligned block of 256 rows (0 to 255, 256 to 511, ..., all dimensions but the last counted through in order) at most 128 rows name the same one
- qkv_weight: bfloat16 [3, 512, 512], P(None, ('dp', 'expert')), may hold values from -0.375 to 0.375
- out_weight: bfloat16 [512, 512], P(('dp', 'expert')), may hold values from -0.375 to 0.375
- router_weight: bfloat16 [512, 8], P(('dp', 'expert')), may hold values from -0.1875 to 0.1875
- norm_gains: bfloat16 [2, 512], P(None, ('dp', 'expert')), may hold values from 0.5 to 1.5
- norm_biases: bfloat16 [2, 512], P(None, ('dp', 'expert')), may hold values from -2 to 2
- expert_in: bfloat16 [8, 512, 2048], P('expert', 'dp'), may hold values from -0.25 to 0.25
- expert_out: bfloat16 [8, 2048, 512], P('expert', 'dp'), may hold values from -1 to 1
- cotangent: bfloat16 [2, 8192, 512], P(None, ('dp', 'expert')), may hold values from -6 to 6
Outputs:
- block_out: bfloat16 [2, 8192, 512], P(None, ('dp', 'expert'))
- input_grad: bfloat16 [2, 8192, 512], P(None, ('dp', 'expert'))
- qkv_grad: float32 [3, 512, 512], P(None, ('dp', 'expert'))
- out_grad: float32 [512, 512], P(('dp', 'expert'))
- router_grad: float32 [512, 8], P(('dp', 'expert'))
- gains_grad: float32 [2, 512], P(None, ('dp', 'expert'))
- biases_grad: float32 [2, 512], P(None, ('dp', 'expert'))
- expert_in_grad: float32 [8, 512, 2048], P('expert', 'dp')
- expert_out_grad: float32 [8, 2048, 512], P('expert', 'dp')
Inputs may be any that keep to these rules, and one draw needn't show every extreme that they name: `image_ids`: along each micro-batch's rows the numbers never fall and start at 0; each image has 1 to 197 rows, some image exactly 197. `routes`: A row names two different experts. Within one micro-batch, the 256 rows held by one device name any one expert at most 128 times, counting both choices; this most is reached.
All inputs are finite; a program needn't handle non-finite values.
Results may differ from a plain program's by a relative error of at most 0.015.
The roundings to bfloat16 on the way count: a program that leaves them out, or rounds other values in their place, can miss the bound.
Values may be sent and summed in bfloat16 or wider, within the bound.
A program may use at most 192 MiB of HBM per device.

v0:
```python
import math

import jax
import jax.numpy as jnp
from jax import lax
from jax.sharding import PartitionSpec as P

D = 512
HEADS = 8
HEAD_DIM = 64
FF = 2048
TOP = 2
IMG = 197
MICRO = 2


neg_big = -1e30
norm_eps = 1e-06
highest = lax.Precision.HIGHEST


def padded(cells, sides, width):
    for axis, dim in sides:
        count = lax.axis_size(axis)
        ends = count - 1
        head = lax.slice_in_dim(cells, 0, width, axis=dim)
        tail = lax.slice_in_dim(cells, cells.shape[dim] - width, cells.shape[dim], axis=dim)
        cells = jnp.concatenate(
            [
                lax.ppermute(tail, axis, [(i, (i + 1) % count) for i in range(ends)]),
                cells,
                lax.ppermute(head, axis, [((i + 1) % count, i) for i in range(ends)]),
            ],
            axis=dim,
        )
    return cells


def layer_norm(values, gain_row, bias_row):
    centre = jnp.mean(values, axis=-1, keepdims=True)
    offset = values - centre
    spread = jnp.mean(offset * offset, axis=-1, keepdims=True)
    return offset * lax.rsqrt(spread + norm_eps) * gain_row + bias_row


def tanh_gelu(values):
    return jax.nn.gelu(values, approximate=True)


def fetch_dense(qkv_weight, out_weight, router_weight, norm_gains, norm_biases):
    return (
        lax.all_gather(qkv_weight, ("dp", "expert"), axis=1, tiled=True),
        lax.all_gather(out_weight, ("dp", "expert"), axis=0, tiled=True),
        lax.all_gather(router_weight, ("dp", "expert"), axis=0, tiled=True),
        lax.all_gather(norm_gains, ("dp", "expert"), axis=1, tiled=True),
        lax.all_gather(norm_biases, ("dp", "expert"), axis=1, tiled=True),
    )


def fetch_experts(expert_in, expert_out):
    return (
        lax.all_gather(expert_in, "dp", axis=1, tiled=True),
        lax.all_gather(expert_out, "dp", axis=1, tiled=True),
    )


def plan_routes(route_ids, shard_experts):
    row_count = route_ids.shape[0]
    experts = shard_experts * lax.axis_size("expert")
    devices = lax.axis_size(("dp", "expert"))
    slot_count = 2 * TOP * row_count // experts
    capacity = 5 * TOP * row_count * devices // (4 * experts)
    labels = lax.broadcasted_iota(jnp.int32, (1, experts), 1)
    first_hot = (route_ids[:, 0:1] == labels).astype(jnp.int32)
    second_hot = (route_ids[:, 1:2] == labels).astype(jnp.int32)
    counts = jnp.stack([jnp.sum(first_hot, axis=0), jnp.sum(second_hot, axis=0)])
    all_counts = lax.all_gather(counts[None], ("dp", "expert"), axis=0, tiled=True)
    earlier = (
        lax.broadcasted_iota(jnp.int32, (devices, 1, 1), 0) < lax.axis_index(("dp", "expert"))
    ).astype(jnp.int32)
    before = jnp.sum(all_counts * earlier, axis=0)
    total_first = jnp.sum(all_counts[:, 0, :], axis=0)
    rank_first = jnp.sum((jnp.cumsum(first_hot, axis=0) - first_hot) * first_hot, axis=1)
    rank_second = jnp.sum((jnp.cumsum(second_hot, axis=0) - second_hot) * second_hot, axis=1)
    place_first = jnp.sum(first_hot * before[0][None, :], axis=1) + rank_first
    place_second = jnp.sum(second_hot * (total_first + before[1])[None, :], axis=1) + rank_second
    kept_mask = jnp.stack([place_first < capacity, place_second < capacity], axis=1)
    slot_second = jnp.sum(second_hot * counts[0][None, :], axis=1) + rank_second
    flat_index = jnp.stack(
        [route_ids[:, 0] * slot_count + rank_first, route_ids[:, 1] * slot_count + slot_second],
        axis=1,
    )
    target = jnp.where(kept_mask, flat_index, experts * slot_count)
    return (first_hot, second_hot, target, kept_mask.astype(jnp.float32))


def fill_slots(row_pairs, target, experts, slot_count):
    feature_count = row_pairs.shape[-1]
    buffer = jnp.zeros((experts * slot_count + 1, feature_count), row_pairs.dtype)
    buffer = buffer.at[target.reshape(-1)].set(row_pairs.reshape(-1, feature_count))
    return buffer[:-1].reshape(experts, 1, slot_count, feature_count)


def read_slots(returned, target):
    feature_count = returned.shape[-1]
    flat_table = jnp.concatenate(
        [returned.reshape(-1, feature_count), jnp.zeros((1, feature_count), returned.dtype)], axis=0
    )
    return flat_table[target]


def run_forward(tokens_f, ids_ext, route_plan, dense_set, expert_set):
    qkv_full, out_full, router_full, gain_pair, bias_pair = dense_set
    expert_up_weight, expert_down_weight = expert_set
    first_hot, second_hot, target, kept_mask = route_plan
    row_count = tokens_f.shape[0]
    rim_rows = IMG - 1
    score_scale = 1.0 / math.sqrt(HEAD_DIM)
    experts = router_full.shape[1]
    slot_count = 2 * TOP * row_count // experts
    normed_one = layer_norm(
        tokens_f, gain_pair[0].astype(jnp.float32), bias_pair[0].astype(jnp.float32)
    ).astype(jnp.bfloat16)
    projected = jnp.einsum(
        "rd,cde->cre", normed_one, qkv_full, preferred_element_type=jnp.float32
    ).astype(jnp.bfloat16)
    key_value = padded(projected[1:], ((("dp", "expert"), 1),), rim_rows)
    query_heads = projected[0].reshape(row_count, HEADS, HEAD_DIM)
    key_heads = key_value[0].reshape(-1, HEADS, HEAD_DIM)
    value_heads = key_value[1].reshape(-1, HEADS, HEAD_DIM)
    same_image = ids_ext[rim_rows : rim_rows + row_count][:, None] == ids_ext[None, :]
    scores = (
        jnp.einsum("qhd,khd->hqk", query_heads, key_heads, preferred_element_type=jnp.float32)
        * score_scale
    )
    scores = jnp.where(same_image[None], scores, neg_big)
    top_score = jnp.max(scores, axis=-1, keepdims=True)
    log_total = top_score + jnp.log(jnp.sum(jnp.exp(scores - top_score), axis=-1, keepdims=True))
    att_probs = jnp.exp(scores - log_total)
    att_low = att_probs.astype(jnp.bfloat16)
    mixed_rows = (
        jnp.einsum("hqk,khd->qhd", att_low, value_heads, preferred_element_type=jnp.float32)
        .reshape(row_count, D)
        .astype(jnp.bfloat16)
    )
    residual = tokens_f + jnp.dot(mixed_rows, out_full, preferred_element_type=jnp.float32)
    normed_two = layer_norm(
        residual, gain_pair[1].astype(jnp.float32), bias_pair[1].astype(jnp.float32)
    ).astype(jnp.bfloat16)
    router_probs = jax.nn.softmax(
        jnp.dot(normed_two, router_full, preferred_element_type=jnp.float32), axis=-1
    )
    picked = jnp.stack(
        [jnp.sum(first_hot * router_probs, axis=1), jnp.sum(second_hot * router_probs, axis=1)],
        axis=1,
    )
    gate_values = kept_mask * picked
    outgoing = fill_slots(
        jnp.broadcast_to(normed_two[:, None, :], (row_count, TOP, D)), target, experts, slot_count
    )
    arrived = lax.all_to_all(outgoing, "expert", split_axis=0, concat_axis=1, tiled=True)
    shard_experts = arrived.shape[0]
    collected_token_rows = arrived.reshape(shard_experts, -1, D)
    hidden_pre = jnp.einsum(
        "ycq,yqt->yct", collected_token_rows, expert_up_weight, preferred_element_type=jnp.float32
    )
    hidden_activation = tanh_gelu(hidden_pre).astype(jnp.bfloat16)
    produced = jnp.einsum(
        "nso,nop->nsp", hidden_activation, expert_down_weight, preferred_element_type=jnp.float32
    ).astype(jnp.bfloat16)
    returned = lax.all_to_all(
        produced.reshape(arrived.shape), "expert", split_axis=1, concat_axis=0, tiled=True
    )
    expert_rows = read_slots(returned, target)
    block_value = residual + jnp.sum(
        gate_values[:, :, None] * expert_rows.astype(jnp.float32), axis=1
    )
    return (
        normed_one,
        query_heads,
        key_heads,
        value_heads,
        att_probs,
        att_low,
        mixed_rows,
        residual,
        normed_two,
        router_probs,
        gate_values,
        collected_token_rows,
        hidden_pre,
        hidden_activation,
        expert_rows,
        block_value,
    )


def run_backward(tokens_f, ids_ext, route_plan, dense_set, expert_set, upstream, gradients):
    qkv_full, out_full, router_full, gain_pair, bias_pair = dense_set
    expert_up_weight, expert_down_weight = expert_set
    first_hot, second_hot, target, kept_mask = route_plan
    grad_qkv, grad_out, grad_router, grad_gains, grad_biases, grad_in, grad_expert_out = gradients
    (
        normed_one,
        query_heads,
        key_heads,
        value_heads,
        att_probs,
        att_low,
        mixed_rows,
        residual,
        normed_two,
        router_probs,
        gate_values,
        collected_token_rows,
        hidden_pre,
        hidden_activation,
        expert_rows,
        block_value,
    ) = run_forward(tokens_f, ids_ext, route_plan, dense_set, expert_set)
    row_count = tokens_f.shape[0]
    rim_rows = IMG - 1
    score_scale = 1.0 / math.sqrt(HEAD_DIM)
    experts = router_full.shape[1]
    slot_count = 2 * TOP * row_count // experts
    shard_experts = expert_up_weight.shape[0]
    d_gate = kept_mask * jnp.sum(upstream[:, None, :] * expert_rows.astype(jnp.float32), axis=-1)
    d_sent = (gate_values[:, :, None] * upstream[:, None, :]).astype(jnp.bfloat16)
    d_arrived = lax.all_to_all(
        fill_slots(d_sent, target, experts, slot_count),
        "expert",
        split_axis=0,
        concat_axis=1,
        tiled=True,
    )
    produced_rows_grad = d_arrived.reshape(shard_experts, -1, D)
    activation_grad = jnp.einsum(
        "tkw,tew->tke", produced_rows_grad, expert_down_weight, preferred_element_type=jnp.float32
    )
    grad_expert_out = grad_expert_out + jnp.einsum(
        "meq,mek->mqk", hidden_activation, produced_rows_grad, preferred_element_type=jnp.float32
    )
    gelu_value, gelu_back = jax.vjp(tanh_gelu, hidden_pre)
    preactivation_grad = gelu_back(activation_grad)[0].astype(jnp.bfloat16)
    grad_in = grad_in + jnp.einsum(
        "zjo,zjm->zom", collected_token_rows, preactivation_grad, preferred_element_type=jnp.float32
    )
    d_rows = jnp.einsum(
        "iht,imt->ihm", preactivation_grad, expert_up_weight, preferred_element_type=jnp.float32
    ).astype(jnp.bfloat16)
    d_back = lax.all_to_all(
        d_rows.reshape(d_arrived.shape), "expert", split_axis=1, concat_axis=0, tiled=True
    )
    d_normed_two = jnp.sum(
        kept_mask[:, :, None] * read_slots(d_back, target).astype(jnp.float32), axis=1
    )
    d_probs = first_hot * d_gate[:, 0:1] + second_hot * d_gate[:, 1:2]
    d_logits = router_probs * (d_probs - jnp.sum(router_probs * d_probs, axis=-1, keepdims=True))
    router_wide = router_full.astype(jnp.float32)
    d_normed_two = d_normed_two + jnp.dot(d_logits, router_wide.T, precision=highest)
    grad_router = grad_router + jnp.dot(
        normed_two.astype(jnp.float32).T, d_logits, precision=highest
    )
    norm_value, second_back = jax.vjp(
        layer_norm, residual, gain_pair[1].astype(jnp.float32), bias_pair[1].astype(jnp.float32)
    )
    d_resid_part, d_gain_two, d_bias_two = second_back(d_normed_two)
    d_resid = upstream + d_resid_part
    d_attn = d_resid.astype(jnp.bfloat16)
    grad_out = grad_out + jnp.einsum(
        "rd,re->de", mixed_rows, d_attn, preferred_element_type=jnp.float32
    )
    d_mixed = (
        jnp.einsum("re,de->rd", d_attn, out_full, preferred_element_type=jnp.float32)
        .astype(jnp.bfloat16)
        .reshape(row_count, HEADS, HEAD_DIM)
    )
    d_att = jnp.einsum("qhd,khd->hqk", d_mixed, value_heads, preferred_element_type=jnp.float32)
    d_scores = (att_probs * (d_att - jnp.sum(att_probs * d_att, axis=-1, keepdims=True))).astype(
        jnp.bfloat16
    )
    d_query = (
        (
            jnp.einsum("hqk,khd->qhd", d_scores, key_heads, preferred_element_type=jnp.float32)
            * score_scale
        )
        .astype(jnp.bfloat16)
        .reshape(row_count, D)
    )
    d_key = (
        jnp.einsum("hqk,qhd->khd", d_scores, query_heads, preferred_element_type=jnp.float32)
        * score_scale
    )
    d_value = jnp.einsum("hqk,qhd->khd", att_low, d_mixed, preferred_element_type=jnp.float32)
    d_pair = jnp.stack([d_key.reshape(-1, D), d_value.reshape(-1, D)])
    rim_grads = jnp.concatenate([d_pair[:, :rim_rows], d_pair[:, rim_rows + row_count :]], axis=1)
    beside_all = padded(rim_grads.astype(jnp.bfloat16), ((("dp", "expert"), 1),), rim_rows).astype(
        rim_grads.dtype
    )
    own_part = d_pair[:, rim_rows : rim_rows + row_count]
    from_below = jnp.pad(beside_all[:, :rim_rows], ((0, 0), (0, row_count - rim_rows), (0, 0)))
    from_above = jnp.pad(beside_all[:, 3 * rim_rows :], ((0, 0), (row_count - rim_rows, 0), (0, 0)))
    d_kv = (own_part + from_below + from_above).astype(jnp.bfloat16)
    d_projected = jnp.concatenate([d_query[None], d_kv], axis=0)
    grad_qkv = grad_qkv + jnp.einsum(
        "rd,cre->cde", normed_one, d_projected, preferred_element_type=jnp.float32
    )
    d_normed_one = jnp.einsum(
        "cre,cde->rd", d_projected, qkv_full, preferred_element_type=jnp.float32
    )
    first_value, first_back = jax.vjp(
        layer_norm, tokens_f, gain_pair[0].astype(jnp.float32), bias_pair[0].astype(jnp.float32)
    )
    d_tokens_part, d_gain_one, d_bias_one = first_back(d_normed_one)
    grad_gains = grad_gains + jnp.stack([d_gain_one, d_gain_two])
    grad_biases = grad_biases + jnp.stack([d_bias_one, d_bias_two])
    input_rows = (d_resid + d_tokens_part).astype(jnp.bfloat16)
    return (
        input_rows,
        (grad_qkv, grad_out, grad_router, grad_gains, grad_biases, grad_in, grad_expert_out),
    )


def body(
    tokens,
    image_ids,
    routes,
    qkv_weight,
    out_weight,
    router_weight,
    norm_gains,
    norm_biases,
    expert_in,
    expert_out,
    cotangent,
):
    shard_experts = expert_in.shape[0]
    rim_rows = IMG - 1
    experts = shard_experts * lax.axis_size("expert")
    outputs = []
    saved_state = []
    for batch_index in range(MICRO):
        dense_set = fetch_dense(qkv_weight, out_weight, router_weight, norm_gains, norm_biases)
        expert_set = fetch_experts(expert_in, expert_out)
        ids_ext = padded(image_ids[batch_index] + 1, ((("dp", "expert"), 0),), rim_rows)
        route_plan = plan_routes(routes[batch_index], shard_experts)
        forward_state = run_forward(
            tokens[batch_index].astype(jnp.float32), ids_ext, route_plan, dense_set, expert_set
        )
        outputs.append(forward_state[-1].astype(jnp.bfloat16))
        saved_state.append((ids_ext, route_plan))
    gradients = (
        jnp.zeros((3, D, D), jnp.float32),
        jnp.zeros((D, D), jnp.float32),
        jnp.zeros((D, experts), jnp.float32),
        jnp.zeros((2, D), jnp.float32),
        jnp.zeros((2, D), jnp.float32),
        jnp.zeros((shard_experts, D, FF), jnp.float32),
        jnp.zeros((shard_experts, FF, D), jnp.float32),
    )
    input_grads = []
    for batch_index in range(MICRO):
        dense_set = fetch_dense(qkv_weight, out_weight, router_weight, norm_gains, norm_biases)
        expert_set = fetch_experts(expert_in, expert_out)
        ids_ext, route_plan = saved_state[batch_index]
        input_rows, gradients = run_backward(
            tokens[batch_index].astype(jnp.float32),
            ids_ext,
            route_plan,
            dense_set,
            expert_set,
            cotangent[batch_index].astype(jnp.float32),
            gradients,
        )
        input_grads.append(input_rows)
    grad_qkv, grad_out, grad_router, grad_gains, grad_biases, grad_in, grad_expert_out = gradients
    dense_grads = (
        lax.psum_scatter(grad_qkv, ("dp", "expert"), scatter_dimension=1, tiled=True),
        lax.psum_scatter(grad_out, ("dp", "expert"), scatter_dimension=0, tiled=True),
        lax.psum_scatter(grad_router, ("dp", "expert"), scatter_dimension=0, tiled=True),
        lax.psum_scatter(grad_gains, ("dp", "expert"), scatter_dimension=1, tiled=True),
        lax.psum_scatter(grad_biases, ("dp", "expert"), scatter_dimension=1, tiled=True),
    )
    expert_grads = (
        lax.psum_scatter(
            grad_in.astype(jnp.bfloat16), "dp", scatter_dimension=1, tiled=True
        ).astype(jnp.float32),
        lax.psum_scatter(
            grad_expert_out.astype(jnp.bfloat16), "dp", scatter_dimension=1, tiled=True
        ).astype(jnp.float32),
    )
    return (
        jnp.stack(outputs),
        jnp.stack(input_grads),
        dense_grads[0],
        dense_grads[1],
        dense_grads[2],
        dense_grads[3],
        dense_grads[4],
        expert_grads[0],
        expert_grads[1],
    )


def solution(mesh):
    return jax.shard_map(
        body,
        mesh=mesh,
        in_specs=(
            P(None, ("dp", "expert"), None),
            P(None, ("dp", "expert")),
            P(None, ("dp", "expert"), None),
            P(None, ("dp", "expert"), None),
            P(("dp", "expert"), None),
            P(("dp", "expert"), None),
            P(None, ("dp", "expert")),
            P(None, ("dp", "expert")),
            P("expert", "dp", None),
            P("expert", "dp", None),
            P(None, ("dp", "expert"), None),
        ),
        out_specs=(
            P(None, ("dp", "expert"), None),
            P(None, ("dp", "expert"), None),
            P(None, ("dp", "expert"), None),
            P(("dp", "expert"), None),
            P(("dp", "expert"), None),
            P(None, ("dp", "expert")),
            P(None, ("dp", "expert")),
            P("expert", "dp", None),
            P("expert", "dp", None),
        ),
        check_vma=False,
    )
```

profile of v0, /device:TPU:0, one launch (start us, length us, event | category | flops | bytes accessed | tf_op | source)
XLA Modules:
  0.0 1657.7 jit_solution(11202165341727803512)
XLA Ops:
  10.8 5.6 collective-permute-start.6
  17.7 4.6 collective-permute-start.2
  24.9 66.6 %all-gather.3 = bf16[32,16,2]{1,2,0:T(2,128)(2,1)S(1)} all-gather(bf16[1,16,2]{1,2,0:T(2,128)(2,1)} %bitcast.529), channel_id=1, replica_groups=mesh['dp'=8,'expert'=4] {'dp','expert'}, dimensions={0}, use_global_device_ids=true | all-gather | bytes 2112 | tf_op jit(solution)/shard_map/all_gather | solution.py:56
  91.6 63.2 %all-gather.2 = bf16[32,16,2]{1,2,0:T(2,128)(2,1)S(1)} all-gather(bf16[1,16,2]{1,2,0:T(2,128)(2,1)} %bitcast.530), channel_id=1, replica_groups=mesh['dp'=8,'expert'=4] {'dp','expert'}, dimensions={0}, use_global_device_ids=true | all-gather | bytes 2112 | tf_op jit(solution)/shard_map/all_gather | solution.py:55
  154.9 69.9 %all_gather.21 = bf16[512,512]{1,0:T(8,128)(2,1)S(1)} all-gather(bf16[16,512]{1,0:T(8,128)(2,1)} %param.15), channel_id=1, replica_groups=mesh['dp'=8,'expert'=4] {'dp','expert'}, dimensions={0}, use_global_device_ids=true | all-gather | bytes 540672 | tf_op jit(solution)/shard_map/all_gather | solution.py:53
  226.7 63.5 %all-gather.4 = s32[32,2,8]{2,1,0:T(2,128)S(1)} all-gather(s32[1,2,8]{2,1,0:T(2,128)S(1)} %add_bitcast_fusion.1), channel_id=2, replica_groups=mesh['dp'=8,'expert'=4] {'dp','expert'}, dimensions={0}, use_global_device_ids=true | all-gather | bytes 2112 | tf_op jit(solution)/shard_map/all_gather | solution.py:77
  290.4 65.7 %all-gather.6 = s32[32,2,8]{2,1,0:T(2,128)S(1)} all-gather(s32[1,2,8]{2,1,0:T(2,128)S(1)} %add_bitcast_fusion.2), channel_id=3, replica_groups=mesh['dp'=8,'expert'=4] {'dp','expert'}, dimensions={0}, use_global_device_ids=true | all-gather | bytes 2112 | tf_op jit(solution)/shard_map/all_gather | solution.py:77
  361.6 64.1 %all-gather.5 = bf16[32,16,8]{1,2,0:T(8,128)(2,1)S(1)} all-gather(bf16[1,16,8]{1,2,0:T(8,128)(2,1)} %bitcast.516), channel_id=1, replica_groups=mesh['dp'=8,'expert'=4] {'dp','expert'}, dimensions={0}, use_global_device_ids=true | all-gather | bytes 8448 | tf_op jit(solution)/shard_map/all_gather | solution.py:54
  434.7 5.5 collective-permute-start.4
  444.5 5.5 collective-permute-start
  450.9 3.2 collective-permute-done.5
  463.2 6.9 collective-permute-done.1
  481.3 4.6 scatter_custom_fusion.2
  488.2 4.3 all-to-all-start.4
  495.6 3.9 scatter_custom_fusion
  501.8 15.4 all-to-all-done.4
  517.2 4.3 all-to-all-start
  523.2 2.9 mul.796
  526.7 3.4 scatter_custom_fusion.3
  531.2 15.6 all-to-all-done
  546.8 4.4 all-to-all-start.6
  553.4 3.2 scatter_custom_fusion.1
  557.7 18.8 %all-to-all-done.6 = bf16[8,1,128,512]{3,2,1,0:T(8,128)(2,1)} async-done(((bf16[8,1,128,512]{3,2,1,0:T(8,128)(2,1)}), bf16[8,1,128,512]{3,2,1,0:T(8,128)(2,1)}, u32[]{:S(2)}, u32[]{:S(2)}) %all-to-all-start.6) | async-done | bytes 1048608 | tf_op jit(solution)/shard_map/all_to_all | solution.py:229
  576.5 4.3 all-to-all-start.2
  587.0 19.0 %all-to-all-done.2 = bf16[8,1,128,512]{3,2,1,0:T(8,128)(2,1)} async-done(((bf16[8,1,128,512]{3,2,1,0:T(8,128)(2,1)}), bf16[8,1,128,512]{3,2,1,0:T(8,128)(2,1)}, u32[]{:S(2)}, u32[]{:S(2)}) %all-to-all-start.2) | async-done | bytes 1048608 | tf_op jit(solution)/shard_map/all_to_all | solution.py:161
  608.3 8.1 fusion.188
  616.4 12.6 fusion.6
  632.5 4.5 all-to-all-start.5
  637.0 7.5 convolution_convert_fusion.3
  645.6 5.6 fusion.189
  651.2 11.0 all-to-all-done.5
  662.2 4.3 all-to-all-start.1
  666.5 12.6 fusion.13
  682.6 9.2 all-to-all-done.1
  691.8 3.9 all-to-all-start.7
  695.7 7.3 convolution_convert_fusion.2
  704.2 16.7 %all-to-all-done.7 = bf16[2,4,128,512]{3,2,0,1:T(8,128)(2,1)S(1)} async-done(((bf16[2,4,128,512]{3,2,0,1:T(8,128)(2,1)}), bf16[2,4,128,512]{3,2,0,1:T(8,128)(2,1)S(1)}, u32[]{:S(2)}, u32[]{:S(2)}) %all-to-all-start.7) | async-done | bytes 1048608 | tf_op jit(solution)/shard_map/all_to_all | solution.py:251
  720.9 4.3 all-to-all-start.3
  755.4 4.1 multiply_reduce_fusion.4
  766.5 3.5 multiply_reduce_fusion.2
  780.5 7.5 multiply_reduce_fusion
  788.1 3.7 fusion.153
  792.3 5.2 fusion.156
  797.6 7.5 multiply_reduce_fusion.1
  806.9 3.2 convolution_multiply_fusion
  816.7 2.9 copy.228
  823.3 5.3 collective-permute-start.10
  828.7 3.0 copy.219
  831.7 3.0 copy.218
  838.9 5.3 collective-permute-start.8
  848.6 6.2 collective-permute-done.9
  865.9 4.5 add_bitcast_fusion
  870.4 5.2 copy.232
  876.0 4.7 fusion.190
  880.7 4.4 add_convert_fusion.1
  885.2 5.8 fusion.169
  891.1 7.6 add_convert_fusion
  903.6 90.0 %reduce-scatter.19.cloned.1.call-done = f32[16,8]{1,0:T(8,128)} async-done(((f32[512,8]{1,0:T(8,128)}), f32[16,8]{1,0:T(8,128)}) %reduce-scatter.19.cloned.1.call-update) | async-done | bytes 528
  996.3 130.3 %reduce-scatter.21.cloned.1.call-done = f32[16,2]{1,0:T(8,128)} async-done(((f32[512,2]{1,0:T(8,128)}), f32[16,2]{1,0:T(8,128)}) %reduce-scatter.21.cloned.1.call-update) | async-done | bytes 144
  1127.9 130.9 %reduce-scatter.23.cloned.1.call-done = f32[16,2]{1,0:T(8,128)} async-done(((f32[512,2]{1,0:T(8,128)}), f32[16,2]{1,0:T(8,128)}) %reduce-scatter.23.cloned.1.call-update) | async-done | bytes 144
  1260.1 143.2 %all-reduce.9.cloned.1.call-done = f32[3,512,512]{2,0,1:T(4,128)} async-done(((f32[3,512,512]{2,0,1:T(4,128)}), f32[3,512,512]{2,0,1:T(4,128)}) %all-reduce.9.cloned.1.call-update) | async-done | bytes 3145744
  1404.9 52.4 %reduce-scatter.15.cloned.1.call-done = bf16[2,64,2048]{2,1,0:T(8,128)(2,1)} async-done(((bf16[2,512,2048]{2,1,0:T(8,128)(2,1)}), bf16[2,64,2048]{2,1,0:T(8,128)(2,1)}) %reduce-scatter.15.cloned.1.call-update) | async-done | bytes 524304 | tf_op jit(solution)/shard_map/reduce_scatter | solution.py:385
  1459.4 52.6 %reduce-scatter.17.cloned.1.call-done = bf16[2,256,512]{2,1,0:T(8,128)(2,1)} async-done(((bf16[2,2048,512]{2,1,0:T(8,128)(2,1)}), bf16[2,256,512]{2,1,0:T(8,128)(2,1)}) %reduce-scatter.17.cloned.1.call-update) | async-done | bytes 524304 | tf_op jit(solution)/shard_map/reduce_scatter | solution.py:388
  1514.1 136.3 %reduce-scatter.13.cloned.1.call-done = f32[16,512]{1,0:T(8,128)} async-done(((f32[512,512]{1,0:T(8,128)}), f32[16,512]{1,0:T(8,128)}) %reduce-scatter.13.cloned.1.call-update) | async-done | bytes 32784 | tf_op jit(solution)/shard_map/reduce_scatter | solution.py:379
  (539 shorter events, 176.6 us)
Async XLA Ops:
  7.2 421.3 %copy-start.3 = (bf16[2,256,512]{2,1,0:T(8,128)(2,1)S(1)}, bf16[2,256,512]{2,1,0:T(8,128)(2,1)}, u32[]{:S(2)}) copy-start(bf16[2,256,512]{2,1,0:T(8,128)(2,1)} %param.11) | copy-start | bytes 1572868
  7.2 421.3 %all-gather.11.cloned.1.call-start = ((), (), s32[]{:S(2)}) async-start(), calls=%async_computation.14 | async-start | bytes 1622016 | tf_op jit(solution)/shard_map/all_gather | solution.py:52
  7.9 600.4 %all-gather.15.cloned.1.call-start = ((), (), s32[]{:S(2)}) async-start(), calls=%async_computation.16 | async-start | bytes 4718592 | tf_op jit(solution)/shard_map/all_gather | solution.py:63
  8.7 607.7 %all-gather.13.cloned.1.call-start = ((), (), s32[]{:S(2)}) async-start(), calls=%async_computation.15 | async-start | bytes 4718592 | tf_op jit(solution)/shard_map/all_gather | solution.py:62
  9.6 418.4 %collective-permute-start.7 = (s32[196]{0:T(256)S(1)}, s32[196]{0:T(256)S(1)}, u32[]{:S(2)}, u32[]{:S(2)}) collective-permute-start(s32[196]{0:T(256)S(1)} %bitcast.528), channel_id=1, source_target_pairs={{1,0},{2,1},{3,2},{4,3},{5,4},{6,5},{7,6},{8,7},{9,8},{10,9},{11,1... | collective-permute-start | bytes 2360 | tf_op jit(solution)/shard_map/ppermute | solution.py:32
  10.8 417.1 %collective-permute-start.6 = (s32[196]{0:T(256)S(1)}, s32[196]{0:T(256)S(1)}, u32[]{:S(2)}, u32[]{:S(2)}) collective-permute-start(s32[196]{0:T(256)S(1)} %bitcast.527), channel_id=1, source_target_pairs={{0,1},{1,2},{2,3},{3,4},{4,5},{5,6},{6,7},{7,8},{8,9},{9,10},{10,1... | collective-permute-start | bytes 2360 | tf_op jit(solution)/shard_map/ppermute | solution.py:30
  16.4 411.8 %collective-permute-start.3 = (s32[196]{0:T(256)S(1)}, s32[196]{0:T(256)S(1)}, u32[]{:S(2)}, u32[]{:S(2)}) collective-permute-start(s32[196]{0:T(256)S(1)} %bitcast.526), channel_id=1, source_target_pairs={{1,0},{2,1},{3,2},{4,3},{5,4},{6,5},{7,6},{8,7},{9,8},{10,9},{11,1... | collective-permute-start | bytes 2360 | tf_op jit(solution)/shard_map/ppermute | solution.py:32
  17.7 410.5 %collective-permute-start.2 = (s32[196]{0:T(256)S(1)}, s32[196]{0:T(256)S(1)}, u32[]{:S(2)}, u32[]{:S(2)}) collective-permute-start(s32[196]{0:T(256)S(1)} %bitcast.525), channel_id=1, source_target_pairs={{0,1},{1,2},{2,3},{3,4},{4,5},{5,6},{6,7},{7,8},{8,9},{9,10},{10,1... | collective-permute-start | bytes 2360 | tf_op jit(solution)/shard_map/ppermute | solution.py:30
  23.5 407.2 %copy-start.81 = (f32[256]{0:T(256)}, f32[256]{0:T(256)S(1)}, u32[]{:S(2)}) copy-start(f32[256]{0:T(256)S(1)} %get-tuple-element.180) | copy-start | bytes 3076
  23.5 416.7 %copy-start.75 = (f32[256]{0:T(256)}, f32[256]{0:T(256)S(1)}, u32[]{:S(2)}) copy-start(f32[256]{0:T(256)S(1)} %get-tuple-element.181) | copy-start | bytes 3076
  24.8 66.6 %copy-start.105 = (f32[256]{0:T(256)}, f32[256]{0:T(256)S(1)}, u32[]{:S(2)}) copy-start(f32[256]{0:T(256)S(1)} %get-tuple-element.75) | copy-start | bytes 3076
  24.8 406.8 %copy-start.107 = (f32[256]{0:T(256)}, f32[256]{0:T(256)S(1)}, u32[]{:S(2)}) copy-start(f32[256]{0:T(256)S(1)} %get-tuple-element.74) | copy-start | bytes 3076
  24.9 406.8 %copy-start.99 = (f32[256]{0:T(256)}, f32[256]{0:T(256)S(1)}, u32[]{:S(2)}) copy-start(f32[256]{0:T(256)S(1)} %fusion.145) | copy-start | bytes 3076
  91.6 348.7 %copy-start.83 = (f32[1,512]{1,0:T(1,128)}, f32[1,512]{1,0:T(1,128)S(1)}, u32[]{:S(2)}) copy-start(f32[1,512]{1,0:T(1,128)S(1)} %get-tuple-element.141) | copy-start | bytes 6148
  154.9 285.3 %copy-start.59 = (f32[1,512]{1,0:T(1,128)}, f32[1,512]{1,0:T(1,128)S(1)}, u32[]{:S(2)}) copy-start(f32[1,512]{1,0:T(1,128)S(1)} %get-tuple-element.139) | copy-start | bytes 6148
  225.5 547.3 %copy-start.61 = (s32[256,1]{0,1:T(1,128)}, s32[256,1]{0,1:T(1,128)S(1)}, u32[]{:S(2)}) copy-start(s32[256,1]{0,1:T(1,128)S(1)} %get-tuple-element.145) | copy-start | bytes 3076
  225.6 547.3 %copy-start.65 = (s32[256,1]{0,1:T(1,128)}, s32[256,1]{0,1:T(1,128)S(1)}, u32[]{:S(2)}) copy-start(s32[256,1]{0,1:T(1,128)S(1)} %get-tuple-element.144) | copy-start | bytes 3076
  290.1 485.5 %copy-start.63 = (s32[256,1]{0,1:T(1,128)}, s32[256,1]{0,1:T(1,128)S(1)}, u32[]{:S(2)}) copy-start(s32[256,1]{0,1:T(1,128)S(1)} %get-tuple-element.146) | copy-start | bytes 3076
  290.1 485.5 %copy-start.67 = (s32[256,1]{0,1:T(1,128)}, s32[256,1]{0,1:T(1,128)S(1)}, u32[]{:S(2)}) copy-start(s32[256,1]{0,1:T(1,128)S(1)} %get-tuple-element.147) | copy-start | bytes 3076
  361.6 64.1 %copy-start.24 = (f32[256,512]{1,0:T(8,128)}, f32[256,512]{1,0:T(8,128)S(1)}, u32[]{:S(2)}) copy-start(f32[256,512]{1,0:T(8,128)S(1)} %get-tuple-element.122) | copy-start | bytes 1572868
  361.6 79.3 %copy-start.85 = (f32[256]{0:T(256)}, f32[256]{0:T(256)S(1)}, u32[]{:S(2)}) copy-start(f32[256]{0:T(256)S(1)} %fusion.143) | copy-start | bytes 3076
  428.2 359.8 %copy-start.18 = (pred[256,648]{0,1:T(8,128)(4,1)}, pred[256,648]{0,1:T(8,128)(4,1)S(1)}, u32[]{:S(2)}) copy-start(pred[256,648]{0,1:T(8,128)(4,1)S(1)} %broadcast_compare_fusion) | copy-start | bytes 497668
  428.4 49.9 %copy-start.20 = (pred[256,648]{0,1:T(8,128)(4,1)}, pred[256,648]{0,1:T(8,128)(4,1)S(1)}, u32[]{:S(2)}) copy-start(pred[256,648]{0,1:T(8,128)(4,1)S(1)} %broadcast_compare_fusion.1) | copy-start | bytes 497668
  433.2 20.8 %copy-start.48 = (bf16[2,256,512]{2,1,0:T(8,128)(2,1)S(1)}, bf16[2,256,512]{2,1,0:T(8,128)(2,1)}, u32[]{:S(2)}) copy-start(bf16[2,256,512]{2,1,0:T(8,128)(2,1)} %slice.349) | copy-start | bytes 1572868
  433.2 20.8 %collective-permute-start.5 = (bf16[2,196,512]{2,1,0:T(8,128)(2,1)}, bf16[2,196,512]{2,1,0:T(8,128)(2,1)}, u32[]{:S(2)}, u32[]{:S(2)}) collective-permute-start(bf16[2,196,512]{2,1,0:T(8,128)(2,1)} %get-tuple-element.119), channel_id=1, source_target_pairs={{1,0},{2,1},{3,2},{4,3},{5,4},{6,5},{7,6},{8,7},{9,8},{10,9},{11,1... | collective-permute-start | bytes 1204232 | tf_op jit(solution)/shard_map/ppermute | solution.py:32
  434.7 19.4 %collective-permute-start.4 = (bf16[2,196,512]{2,1,0:T(8,128)(2,1)}, bf16[2,196,512]{2,1,0:T(8,128)(2,1)}, u32[]{:S(2)}, u32[]{:S(2)}) collective-permute-start(bf16[2,196,512]{2,1,0:T(8,128)(2,1)} %get-tuple-element.118), channel_id=1, source_target_pairs={{0,1},{1,2},{2,3},{3,4},{4,5},{5,6},{6,7},{7,8},{8,9},{9,10},{10,1... | collective-permute-start | bytes 1204232 | tf_op jit(solution)/shard_map/ppermute | solution.py:30
  440.9 17.7 %copy-start.39 = (bf16[3,256,512]{2,1,0:T(8,128)(2,1)}, bf16[3,256,512]{2,1,0:T(8,128)(2,1)S(1)}, u32[]{:S(2)}) copy-start(bf16[3,256,512]{2,1,0:T(8,128)(2,1)S(1)} %fusion.20) | copy-start | bytes 2359300
  442.2 17.8 %copy-start.42 = (bf16[1,256,512]{1,2,0:T(8,128)(2,1)}, bf16[1,256,512]{1,2,0:T(8,128)(2,1)S(1)}, u32[]{:S(2)}) copy-start(bf16[1,256,512]{1,2,0:T(8,128)(2,1)S(1)} %copy.204) | copy-start | bytes 786436
  443.2 26.8 %collective-permute-start.1 = (bf16[2,196,512]{2,1,0:T(8,128)(2,1)}, bf16[2,196,512]{2,1,0:T(8,128)(2,1)}, u32[]{:S(2)}, u32[]{:S(2)}) collective-permute-start(bf16[2,196,512]{2,1,0:T(8,128)(2,1)} %get-tuple-element.117), channel_id=1, source_target_pairs={{1,0},{2,1},{3,2},{4,3},{5,4},{6,5},{7,6},{8,7},{9,8},{10,9},{11,1... | collective-permute-start | bytes 1204232 | tf_op jit(solution)/shard_map/ppermute | solution.py:32
  444.5 25.5 %collective-permute-start = (bf16[2,196,512]{2,1,0:T(8,128)(2,1)}, bf16[2,196,512]{2,1,0:T(8,128)(2,1)}, u32[]{:S(2)}, u32[]{:S(2)}) collective-permute-start(bf16[2,196,512]{2,1,0:T(8,128)(2,1)} %get-tuple-element.116), channel_id=1, source_target_pairs={{0,1},{1,2},{2,3},{3,4},{4,5},{5,6},{6,7},{7,8},{8,9},{9,10},{10,1... | collective-permute-start | bytes 1204232 | tf_op jit(solution)/shard_map/ppermute | solution.py:30
  461.1 326.9 %copy-start.55 = (f32[8,256]{1,0:T(8,128)}, f32[8,256]{1,0:T(8,128)S(1)}, u32[]{:S(2)}) copy-start(f32[8,256]{1,0:T(8,128)S(1)} %log_add_fusion) | copy-start | bytes 24580
  478.3 319.2 %copy-start.57 = (f32[8,256]{1,0:T(8,128)}, f32[8,256]{1,0:T(8,128)S(1)}, u32[]{:S(2)}) copy-start(f32[8,256]{1,0:T(8,128)S(1)} %log_add_fusion.1) | copy-start | bytes 24580
  480.7 21.1 %copy-start.33 = (bf16[256,512]{1,0:T(8,128)(2,1)}, bf16[256,512]{1,0:T(8,128)(2,1)S(1)}, u32[]{:S(2)}) copy-start(bf16[256,512]{1,0:T(8,128)(2,1)S(1)} %get-tuple-element.124) | copy-start | bytes 786436
  480.7 45.4 %copy-start.31 = (bf16[256,512]{1,0:T(8,128)(2,1)}, bf16[256,512]{1,0:T(8,128)(2,1)S(1)}, u32[]{:S(2)}) copy-start(bf16[256,512]{1,0:T(8,128)(2,1)S(1)} %get-tuple-element.125) | copy-start | bytes 786436
  480.9 292.0 %copy-start.69 = (f32[256]{0:T(256)}, f32[256]{0:T(256)S(1)}, u32[]{:S(2)}) copy-start(f32[256]{0:T(256)S(1)} %get-tuple-element.170) | copy-start | bytes 3076
  480.9 291.9 %copy-start.77 = (f32[256]{0:T(256)}, f32[256]{0:T(256)S(1)}, u32[]{:S(2)}) copy-start(f32[256]{0:T(256)S(1)} %fusion.115) | copy-start | bytes 3076
  485.9 35.9 %copy-start.23 = (f32[256,512]{1,0:T(8,128)S(1)}, f32[256,512]{1,0:T(8,128)}, u32[]{:S(2)}) copy-start(f32[256,512]{1,0:T(8,128)} %get-tuple-element.123) | copy-start | bytes 1572868
  488.2 29.0 %all-to-all-start.4 = ((bf16[8,1,128,512]{3,2,1,0:T(8,128)(2,1)}), bf16[8,1,128,512]{3,2,1,0:T(8,128)(2,1)}, u32[]{:S(2)}, u32[]{:S(2)}) async-start(bf16[8,1,128,512]{3,2,1,0:T(8,128)(2,1)} %bitcast.406), calls=%async_computation.4 | async-start | bytes 2097152 | tf_op jit(solution)/shard_map/all_to_all | solution.py:229
  517.2 29.5 %all-to-all-start = ((bf16[8,1,128,512]{3,2,1,0:T(8,128)(2,1)}), bf16[8,1,128,512]{3,2,1,0:T(8,128)(2,1)}, u32[]{:S(2)}, u32[]{:S(2)}) async-start(bf16[8,1,128,512]{3,2,1,0:T(8,128)(2,1)} %bitcast.405), calls=%async_computation | async-start | bytes 2097152 | tf_op jit(solution)/shard_map/all_to_all | solution.py:161
  526.3 249.4 %copy-start.71 = (f32[256]{0:T(256)}, f32[256]{0:T(256)S(1)}, u32[]{:S(2)}) copy-start(f32[256]{0:T(256)S(1)} %get-tuple-element.166) | copy-start | bytes 3076
  526.3 249.4 %copy-start.79 = (f32[256]{0:T(256)}, f32[256]{0:T(256)S(1)}, u32[]{:S(2)}) copy-start(f32[256]{0:T(256)S(1)} %fusion.117) | copy-start | bytes 3076
  546.8 29.7 %all-to-all-start.6 = ((bf16[8,1,128,512]{3,2,1,0:T(8,128)(2,1)}), bf16[8,1,128,512]{3,2,1,0:T(8,128)(2,1)}, u32[]{:S(2)}, u32[]{:S(2)}) async-start(bf16[8,1,128,512]{3,2,1,0:T(8,128)(2,1)} %bitcast.407), calls=%async_computation.6 | async-start | bytes 2097152 | tf_op jit(solution)/shard_map/all_to_all | solution.py:229
  576.5 29.6 %all-to-all-start.2 = ((bf16[8,1,128,512]{3,2,1,0:T(8,128)(2,1)}), bf16[8,1,128,512]{3,2,1,0:T(8,128)(2,1)}, u32[]{:S(2)}, u32[]{:S(2)}) async-start(bf16[8,1,128,512]{3,2,1,0:T(8,128)(2,1)} %bitcast.408), calls=%async_computation.2 | async-start | bytes 2097152 | tf_op jit(solution)/shard_map/all_to_all | solution.py:161
  584.3 32.1 %copy-start.16 = (bf16[2,4,1,128,512]{4,3,1,0,2:T(8,128)(2,1)}, bf16[2,4,1,128,512]{4,3,1,0,2:T(8,128)(2,1)S(1)}, u32[]{:S(2)}) copy-start(bf16[2,4,1,128,512]{4,3,1,0,2:T(8,128)(2,1)S(1)} %copy.200) | copy-start | bytes 3145732
  632.5 29.7 %all-to-all-start.5 = ((bf16[2,4,128,512]{3,2,0,1:T(8,128)(2,1)}), bf16[2,4,128,512]{3,2,0,1:T(8,128)(2,1)}, u32[]{:S(2)}, u32[]{:S(2)}) async-start(bf16[2,4,128,512]{3,2,0,1:T(8,128)(2,1)} %copy.215), calls=%async_computation.5 | async-start | bytes 2097152 | tf_op jit(solution)/shard_map/all_to_all | solution.py:251
  645.6 20.9 %copy-start.27 = (bf16[2,4,1,128,512]{4,3,1,0,2:T(8,128)(2,1)S(1)}, bf16[2,4,1,128,512]{4,3,1,0,2:T(8,128)(2,1)}, u32[]{:S(2)}) copy-start(bf16[2,4,1,128,512]{4,3,1,0,2:T(8,128)(2,1)} %copy.209) | copy-start | bytes 3145732
  662.2 29.6 %all-to-all-start.1 = ((bf16[2,4,128,512]{3,2,0,1:T(8,128)(2,1)}), bf16[2,4,128,512]{3,2,0,1:T(8,128)(2,1)}, u32[]{:S(2)}, u32[]{:S(2)}) async-start(bf16[2,4,128,512]{3,2,0,1:T(8,128)(2,1)} %copy.201), calls=%async_computation.1 | async-start | bytes 2097152 | tf_op jit(solution)/shard_map/all_to_all | solution.py:171
  691.8 29.1 %all-to-all-start.7 = ((bf16[2,4,128,512]{3,2,0,1:T(8,128)(2,1)}), bf16[2,4,128,512]{3,2,0,1:T(8,128)(2,1)S(1)}, u32[]{:S(2)}, u32[]{:S(2)}) async-start(bf16[2,4,128,512]{3,2,0,1:T(8,128)(2,1)} %copy.224), calls=%async_computation.7 | async-start | bytes 2097152 | tf_op jit(solution)/shard_map/all_to_all | solution.py:251
  720.9 38.8 %all-to-all-start.3 = ((bf16[2,4,128,512]{3,2,0,1:T(8,128)(2,1)}), bf16[2,4,128,512]{3,2,0,1:T(8,128)(2,1)}, u32[]{:S(2)}, u32[]{:S(2)}) async-start(bf16[2,4,128,512]{3,2,0,1:T(8,128)(2,1)} %copy.210), calls=%async_computation.3 | async-start | bytes 2097152 | tf_op jit(solution)/shard_map/all_to_all | solution.py:171
  725.2 268.4 %reduce-scatter.19.cloned.1.call-start = ((), (), s32[]{:S(2)}) async-start(), calls=%async_computation.20 | async-start | bytes 270336
  788.1 17.0 %slice-start.6 = ((s8[5308416]{0:T(1024)(128)(4,1)}), s8[1114112]{0:T(1024)(128)(4,1)S(1)}, s32[]{:S(2)}) async-start(s8[5308416]{0:T(1024)(128)(4,1)} %bitcast.390), calls=%async_computation.30 | async-start | bytes 2228224
  822.0 25.4 %collective-permute-start.11 = (bf16[2,196,512]{2,1,0:T(8,128)(2,1)}, bf16[2,196,512]{2,1,0:T(8,128)(2,1)}, u32[]{:S(2)}, u32[]{:S(2)}) collective-permute-start(bf16[2,196,512]{2,1,0:T(8,128)(2,1)} %get-tuple-element.107), channel_id=1, source_target_pairs={{1,0},{2,1},{3,2},{4,3},{5,4},{6,5},{7,6},{8,7},{9,8},{10,9},{11,1... | collective-permute-start | bytes 1204232 | tf_op jit(solution)/shard_map/ppermute | solution.py:32
  823.3 24.2 %collective-permute-start.10 = (bf16[2,196,512]{2,1,0:T(8,128)(2,1)S(1)}, bf16[2,196,512]{2,1,0:T(8,128)(2,1)}, u32[]{:S(2)}, u32[]{:S(2)}) collective-permute-start(bf16[2,196,512]{2,1,0:T(8,128)(2,1)S(1)} %get-tuple-element.106), channel_id=1, source_target_pairs={{0,1},{1,2},{2,3},{3,4},{4,5},{5,6},{6,7},{7,8},{8,9},{9,10},{10,1... | collective-permute-start | bytes 1204232 | tf_op jit(solution)/shard_map/ppermute | solution.py:30
  828.6 15.6 copy-start.88
  836.6 19.3 %copy-start.113 = (pred[256]{0:T(512)(128)(4,1)S(1)}, pred[256]{0:T(512)(128)(4,1)}, u32[]{:S(2)}) copy-start(pred[256]{0:T(512)(128)(4,1)} %constant.98.clone.1) | copy-start | bytes 772
  837.6 17.1 %collective-permute-start.9 = (bf16[2,196,512]{2,1,0:T(8,128)(2,1)}, bf16[2,196,512]{2,1,0:T(8,128)(2,1)}, u32[]{:S(2)}, u32[]{:S(2)}) collective-permute-start(bf16[2,196,512]{2,1,0:T(8,128)(2,1)} %get-tuple-element.109), channel_id=1, source_target_pairs={{1,0},{2,1},{3,2},{4,3},{5,4},{6,5},{7,6},{8,7},{9,8},{10,9},{11,1... | collective-permute-start | bytes 1204232 | tf_op jit(solution)/shard_map/ppermute | solution.py:32
  838.9 15.8 collective-permute-start.8
  847.4 279.2 %reduce-scatter.21.cloned.1.call-start = ((), (), s32[]{:S(2)}) async-start(), calls=%async_computation.21 | async-start | bytes 270336
  864.9 393.9 %reduce-scatter.23.cloned.1.call-start = ((), (), s32[]{:S(2)}) async-start(), calls=%async_computation.22 | async-start | bytes 270336
  865.9 537.4 %all-reduce.9.cloned.1.call-start = ((), (), s32[]{:S(2)}) async-start(), calls=%async_computation.23 | async-start | bytes 8388608
  875.6 581.6 %reduce-scatter.15.cloned.1.call-start = ((), (), s32[]{:S(2)}) async-start(), calls=%async_computation.18 | async-start | bytes 4718592 | tf_op jit(solution)/shard_map/reduce_scatter | solution.py:385
  885.1 626.8 %reduce-scatter.17.cloned.1.call-start = ((), (), s32[]{:S(2)}) async-start(), calls=%async_computation.19 | async-start | bytes 4718592 | tf_op jit(solution)/shard_map/reduce_scatter | solution.py:388
  898.7 96.2 %copy-start.47 = (f32[256,512]{1,0:T(8,128)S(1)}, f32[256,512]{1,0:T(8,128)}, u32[]{:S(2)}) copy-start(f32[256,512]{1,0:T(8,128)} %copy-done.46) | copy-start | bytes 1572868
  898.7 751.7 %reduce-scatter.13.cloned.1.call-start = ((), (), s32[]{:S(2)}) async-start(), calls=%async_computation.17 | async-start | bytes 1081344 | tf_op jit(solution)/shard_map/reduce_scatter | solution.py:379
  (93 other events, 675.2 us)
Sparse Core Ops, SparseCore 0:
  11.0 57.7 all-gather.10
  70.7 35.5 all-gather.14
  108.2 36.7 all-gather.12
  847.5 145.9 reduce-scatter.18
  995.7 130.7 reduce-scatter.20
  1128.6 130.1 reduce-scatter.22
  1265.3 138.0 all-reduce.8
  1407.0 50.1 reduce-scatter.14
  1460.6 51.2 reduce-scatter.16
  1514.7 135.6 reduce-scatter.12
where the time goes:
time: 1670 us; the launch traced here: 1660 us
  waiting for transfers between devices  859 us (51%)
  blocking collectives  393 us (24%)
  matrix products  135 us (8%)
  local copies, waits for them, and re-layouts  119 us (7%)
  starting transfers between devices  74.4 us (4%)
  other arithmetic  59.8 us (4%)
  between operations  17 us (1%)
    unnamed x14, waiting for transfers between devices  496 us
    reduce_scatter x1, waiting for transfers between devices, body(): lax.psum_scatter(grad_out, ('dp', 'expert'), scatter_dimension=0, tiled=T...  136 us
    all_gather x2, blocking collectives, plan_routes(): lax.all_gather(counts[None], ('dp', 'expert'), axis=0, tiled=True)  129 us
    all_gather x1, blocking collectives, fetch_dense(): lax.all_gather(out_weight, ('dp', 'expert'), axis=0, tiled=True)  69.9 us
    all_gather x1, blocking collectives, fetch_dense(): lax.all_gather(norm_biases, ('dp', 'expert'), axis=1, tiled=True)  66.6 us
    all_gather x1, blocking collectives, fetch_dense(): lax.all_gather(router_weight, ('dp', 'expert'), axis=0, tiled=True)  64.1 us
    all_gather x1, blocking collectives, fetch_dense(): lax.all_gather(norm_gains, ('dp', 'expert'), axis=1, tiled=True)  63.2 us
    reduce_scatter x1, waiting for transfers between devices, body(): lax.psum_scatter(grad_expert_out.astype(jnp.bfloat16), 'dp', scatter_dime...  52.6 us
  transfers between devices with their start and end apart: 30, of which 17 were waited for; matrix products, arithmetic and copies ran while one was open for 14% of the time, Pallas kernels for 0%

commit v1 on v0

--- a/solution.py
+++ b/solution.py
@@ -48,12 +48,17 @@
 
 
 def fetch_dense(qkv_weight, out_weight, router_weight, norm_gains, norm_biases):
+    rows, experts = router_weight.shape
+    small = jnp.concatenate([router_weight, norm_gains.T, norm_biases.T], axis=1)
+    small = jnp.pad(small, ((0, 0), (0, D - experts - 4)))
+    packed = jnp.concatenate([qkv_weight, out_weight[None], small[None]], axis=0)
+    full = lax.all_gather(packed, ("dp", "expert"), axis=1, tiled=True)
     return (
-        lax.all_gather(qkv_weight, ("dp", "expert"), axis=1, tiled=True),
-        lax.all_gather(out_weight, ("dp", "expert"), axis=0, tiled=True),
-        lax.all_gather(router_weight, ("dp", "expert"), axis=0, tiled=True),
-        lax.all_gather(norm_gains, ("dp", "expert"), axis=1, tiled=True),
-        lax.all_gather(norm_biases, ("dp", "expert"), axis=1, tiled=True),
+        full[:3],
+        full[3],
+        full[4][:, :experts],
+        full[4][:, experts : experts + 2].T,
+        full[4][:, experts + 2 : experts + 4].T,
     )
 
 
@@ -80,8 +85,17 @@
     ).astype(jnp.int32)
     before = jnp.sum(all_counts * earlier, axis=0)
     total_first = jnp.sum(all_counts[:, 0, :], axis=0)
-    rank_first = jnp.sum((jnp.cumsum(first_hot, axis=0) - first_hot) * first_hot, axis=1)
-    rank_second = jnp.sum((jnp.cumsum(second_hot, axis=0) - second_hot) * second_hot, axis=1)
+    row_before = (
+        lax.broadcasted_iota(jnp.int32, (row_count, row_count), 0)
+        > lax.broadcasted_iota(jnp.int32, (row_count, row_count), 1)
+    ).astype(jnp.bfloat16)
+
+    def rank_of(hot):
+        ahead = jnp.dot(row_before, hot.astype(jnp.bfloat16), preferred_element_type=jnp.float32)
+        return jnp.sum(ahead.astype(jnp.int32) * hot, axis=1)
+
+    rank_first = rank_of(first_hot)
+    rank_second = rank_of(second_hot)
     place_first = jnp.sum(first_hot * before[0][None, :], axis=1) + rank_first
     place_second = jnp.sum(second_hot * (total_first + before[1])[None, :], axis=1) + rank_second
     kept_mask = jnp.stack([place_first < capacity, place_second < capacity], axis=1)
@@ -374,12 +388,16 @@
         )
         input_grads.append(input_rows)
     grad_qkv, grad_out, grad_router, grad_gains, grad_biases, grad_in, grad_expert_out = gradients
+    small = jnp.concatenate([grad_router, grad_gains.T, grad_biases.T], axis=1)
+    small = jnp.pad(small, ((0, 0), (0, D - experts - 4)))
+    packed = jnp.concatenate([grad_qkv, grad_out[None], small[None]], axis=0)
+    packed = lax.psum_scatter(packed, ("dp", "expert"), scatter_dimension=1, tiled=True)
     dense_grads = (
-        lax.psum_scatter(grad_qkv, ("dp", "expert"), scatter_dimension=1, tiled=True),
-        lax.psum_scatter(grad_out, ("dp", "expert"), scatter_dimension=0, tiled=True),
-        lax.psum_scatter(grad_router, ("dp", "expert"), scatter_dimension=0, tiled=True),
-        lax.psum_scatter(grad_gains, ("dp", "expert"), scatter_dimension=1, tiled=True),
-        lax.psum_scatter(grad_biases, ("dp", "expert"), scatter_dimension=1, tiled=True),
+        packed[:3],
+        packed[3],
+        packed[4][:, :experts],
+        packed[4][:, experts : experts + 2].T,
+        packed[4][:, experts + 2 : experts + 4].T,
     )
     expert_grads = (
         lax.psum_scatter(

time: 1670 us -> 859 us (0.51)
  waiting for transfers between devices: 859 us -> 307 us
  blocking collectives: 393 us -> 130 us
    unnamed x14 -> x6, waiting for transfers between devices: 496 us -> 0.78 us
    all_gather x4 -> x0, blocking collectives: 264 us -> none  [the longest x1 69.9 us: fetch_dense(): lax.all_gather(out_weight, ('dp', 'expert'), axis=0, tiled=True)]
    reduce_scatter x1, waiting for transfers between devices: 136 us -> 195 us  [body(): lax.psum_scatter(packed, ('dp', 'expert'), scatter_dimension=1, tiled=True)]
    reduce_scatter x1, waiting for transfers between devices: 52.6 us -> 0.01 us  [body(): lax.psum_scatter(grad_expert_out.astype(jnp.bfloat16), 'dp', scatter_dime...]
    reduce_scatter x1, waiting for transfers between devices: 52.4 us -> 0.01 us  [body(): lax.psum_scatter(grad_in.astype(jnp.bfloat16), 'dp', scatter_dimension=1,...]
    all_to_all x2, waiting for transfers between devices: 27.7 us -> 6.66 us  [run_backward(): lax.all_to_all(d_rows.reshape(d_arrived.shape), 'expert', split_axis=1, c...]
  transfers between devices with their start and end apart: 30 -> 26, of which waited for: 17 -> 11; matrix products, arithmetic and copies ran while one was open for 14% -> 34% of each run, Pallas kernels for 0% -> 0%
where the time goes in v1:
time: 859 us; the launch traced here: 851 us
  waiting for transfers between devices  307 us (36%)
  matrix products  144 us (17%)
  blocking collectives  130 us (15%)
  local copies, waits for them, and re-layouts  115 us (13%)
  starting transfers between devices  73.7 us (9%)
  other arithmetic  64.6 us (8%)
  between operations  17 us (2%)
    reduce_scatter x1, waiting for transfers between devices, body(): lax.psum_scatter(packed, ('dp', 'expert'), scatter_dimension=1, tiled=True)  195 us
    all_gather x2, blocking collectives, plan_routes(): lax.all_gather(counts[None], ('dp', 'expert'), axis=0, tiled=True)  130 us
    all_to_all x2, waiting for transfers between devices, run_backward(): lax.all_to_all(fill_slots(d_sent, target, experts, slot_count), 'expert',...  38.1 us
    all_to_all x2, waiting for transfers between devices, run_forward(): lax.all_to_all(outgoing, 'expert', split_axis=0, concat_axis=1, tiled=True)  36.3 us
    ppermute x6, starting transfers between devices, padded(): lax.ppermute(tail, axis, [(i, (i + 1) % count) for i in range(ends)])  31.8 us
    dot_general x2, matrix products, run_forward(): jnp.einsum('ycq,yqt->yct', collected_token_rows, expert_up_weight, prefer...  23.5 us
    dot_general x2, matrix products, run_backward(): jnp.einsum('meq,mek->mqk', hidden_activation, produced_rows_grad, preferr...  19.2 us
  transfers between devices with their start and end apart: 26, of which 11 were waited for; matrix products, arithmetic and copies ran while one was open for 34% of the time, Pallas kernels for 0%

profile of v1, /device:TPU:0, one launch (start us, length us, event | category | flops | bytes accessed | tf_op | source)
XLA Modules:
  0.0 851.0 jit_solution(2875117579403851115)
XLA Ops:
  14.0 5.6 collective-permute-start.6
  20.8 4.6 collective-permute-start.2
  30.0 66.9 %all-gather.2 = s32[32,2,8]{2,1,0:T(2,128)S(1)} all-gather(s32[1,2,8]{2,1,0:T(2,128)S(1)} %add_bitcast_fusion.1), channel_id=2, replica_groups=mesh['dp'=8,'expert'=4] {'dp','expert'}, dimensions={0}, use_global_device_ids=true | all-gather | bytes 2112 | tf_op jit(solution)/shard_map/all_gather | solution.py:82
  97.0 63.5 %all-gather.3 = s32[32,2,8]{2,1,0:T(2,128)S(1)} all-gather(s32[1,2,8]{2,1,0:T(2,128)S(1)} %add_bitcast_fusion.2), channel_id=3, replica_groups=mesh['dp'=8,'expert'=4] {'dp','expert'}, dimensions={0}, use_global_device_ids=true | all-gather | bytes 2112 | tf_op jit(solution)/shard_map/all_gather | solution.py:82
  173.2 5.6 collective-permute-start.4
  182.0 5.5 collective-permute-start
  188.3 4.2 collective-permute-done.5
  201.9 6.7 collective-permute-done.1
  222.6 3.8 scatter_custom_fusion.2
  227.5 4.3 all-to-all-start.4
  234.1 3.2 scatter_custom_fusion
  238.3 18.3 %all-to-all-done.4 = bf16[8,1,128,512]{3,2,1,0:T(8,128)(2,1)} async-done(((bf16[8,1,128,512]{3,2,1,0:T(8,128)(2,1)}), bf16[8,1,128,512]{3,2,1,0:T(8,128)(2,1)}, u32[]{:S(2)}, u32[]{:S(2)}) %all-to-all-start.4) | async-done | bytes 1048608 | tf_op jit(solution)/shard_map/all_to_all | solution.py:243
  256.6 4.2 all-to-all-start
  264.8 3.4 scatter_custom_fusion.3
  269.3 16.9 %all-to-all-done = bf16[8,1,128,512]{3,2,1,0:T(8,128)(2,1)} async-done(((bf16[8,1,128,512]{3,2,1,0:T(8,128)(2,1)}), bf16[8,1,128,512]{3,2,1,0:T(8,128)(2,1)}, u32[]{:S(2)}, u32[]{:S(2)}) %all-to-all-start) | async-done | bytes 1048608 | tf_op jit(solution)/shard_map/all_to_all | solution.py:175
  286.2 4.2 all-to-all-start.6
  291.7 3.2 scatter_custom_fusion.1
  295.9 19.7 %all-to-all-done.6 = bf16[8,1,128,512]{3,2,1,0:T(8,128)(2,1)} async-done(((bf16[8,1,128,512]{3,2,1,0:T(8,128)(2,1)}), bf16[8,1,128,512]{3,2,1,0:T(8,128)(2,1)}, u32[]{:S(2)}, u32[]{:S(2)}) %all-to-all-start.6) | async-done | bytes 1048608 | tf_op jit(solution)/shard_map/all_to_all | solution.py:243
  315.7 4.4 all-to-all-start.2
  326.0 19.4 %all-to-all-done.2 = bf16[8,1,128,512]{3,2,1,0:T(8,128)(2,1)} async-done(((bf16[8,1,128,512]{3,2,1,0:T(8,128)(2,1)}), bf16[8,1,128,512]{3,2,1,0:T(8,128)(2,1)}, u32[]{:S(2)}, u32[]{:S(2)}) %all-to-all-start.2) | async-done | bytes 1048608 | tf_op jit(solution)/shard_map/all_to_all | solution.py:175
  347.7 8.1 fusion.209
  355.8 12.5 %fusion.6 = (bf16[2,512,2048]{2,1,0:T(8,128)(2,1)S(1)}, f32[2,512,2048]{2,1,0:T(8,128)}) fusion(f32[2,512,2048]{2,1,0:T(8,128)} %fusion.209, bf16[2,512,512]{2,1,0:T(8,128)(2,1)S(1)} %bitcast.379, bf16[2,512,2048]{2,1,0:T(8,128)(2,1)} %all-gather.10.cloned.1.call-done), kind=kOutput, calls=%fused_computation.18 | convolution fusion | flops 2189426688 | bytes 26214400 | tf_op jit(solution)/shard_map/ycq,yqt->yct/dot_general | solution.py:178
  368.3 5.7 fusion.211
  374.0 2.4 convolution_convert_fusion.1
  377.5 3.5 all-to-all-start.5
  381.0 5.0 fusion.210
  386.1 11.1 %fusion.13 = (bf16[2,512,2048]{2,1,0:T(8,128)(2,1)S(1)}, f32[2,512,2048]{2,1,0:T(8,128)}) fusion(f32[2,512,2048]{2,1,0:T(8,128)S(1)} %fusion.210, bf16[2,512,512]{2,1,0:T(8,128)(2,1)S(1)} %bitcast.385, bf16[2,512,2048]{2,1,0:T(8,128)(2,1)} %all-gather.10.cloned.1.call-done), kind=kOutput, calls=%fused_computation.25 | convolution fusion | flops 2189426688 | bytes 26214400 | tf_op jit(solution)/shard_map/ycq,yqt->yct/dot_general | solution.py:178
  399.1 4.4 add_convert_fusion.1
  406.1 7.3 convolution_convert_fusion.3
  414.6 5.0 all-to-all-start.1
  419.9 6.7 convolution_convert_fusion
  427.7 16.6 %all-to-all-done.1 = bf16[2,4,128,512]{3,2,0,1:T(8,128)(2,1)} async-done(((bf16[2,4,128,512]{3,2,0,1:T(8,128)(2,1)}), bf16[2,4,128,512]{3,2,0,1:T(8,128)(2,1)}, u32[]{:S(2)}, u32[]{:S(2)}) %all-to-all-start.1) | async-done | bytes 1048608 | tf_op jit(solution)/shard_map/all_to_all | solution.py:185
  444.3 3.9 all-to-all-start.7
  448.3 7.5 convolution_convert_fusion.2
  456.9 9.9 %fusion.189 = f32[2,2048,512]{2,1,0:T(8,128)} fusion(bf16[2,512,512]{2,1,0:T(8,128)(2,1)S(1)} %bitcast.396, f32[2,512,2048]{2,1,0:T(8,128)} %get-tuple-element.173), kind=kOutput, calls=%fused_computation.394 | convolution fusion | flops 2166358016 | bytes 17825792 | tf_op jit(solution)/shard_map/meq,mek->mqk/dot_general | solution.py:254
  466.8 6.7 all-to-all-done.7
  473.4 4.2 all-to-all-start.3
  477.7 9.3 %add_convert_fusion = bf16[2,2048,512]{2,1,0:T(8,128)(2,1)} fusion(f32[2,2048,512]{2,1,0:T(8,128)} %fusion.189, bf16[2,512,512]{2,1,0:T(8,128)(2,1)} %bitcast.394, f32[2,512,2048]{2,1,0:T(8,128)} %get-tuple-element.169), kind=kOutput, calls=%fused_computation.26 | convolution fusion | flops 2170552320 | bytes 22020096 | tf_op jit(solution)/shard_map/meq,mek->mqk/dot_general | solution.py:254
  488.4 2.8 gather_fusion.2
  491.2 2.7 reshape.919
  495.1 2.6 gather_fusion
  497.8 2.7 reshape.917
  501.7 2.6 gather_fusion.3
  504.4 2.8 reshape.920
  507.1 4.1 multiply_reduce_fusion.4
  513.4 2.6 gather_fusion.1
  516.1 2.8 reshape.918
  518.9 3.8 multiply_reduce_fusion.2
  522.9 2.6 multiply_reduce_fusion.5
  530.1 2.4 multiply_reduce_fusion.8
  537.1 7.7 multiply_reduce_fusion
  544.8 2.6 fusion.173
  549.0 5.2 fusion.176
  554.3 7.1 multiply_reduce_fusion.1
  565.3 2.9 copy.246
  568.2 2.9 copy.247
  575.3 5.3 collective-permute-start.10
  580.7 2.9 copy.238
  583.6 5.5 multiply_convert_fusion.3
  592.8 3.0 copy.237
  600.4 5.3 collective-permute-start.8
  622.5 2.9 pad_maximum_fusion
  625.4 9.2 %copy.253 = f32[5,512,512]{2,0,1:T(8,128)} copy(f32[5,512,512]{1,2,0:T(8,128)} %pad_maximum_fusion) | data formatting | bytes 10485760 | tf_op jit(solution)/shard_map/concatenate | solution.py:393
  643.0 195.4 %reduce-scatter.4.cloned.1.call-done = f32[5,16,512]{2,0,1:T(8,128)} async-done(((f32[5,512,512]{2,0,1:T(8,128)}), f32[5,16,512]{2,0,1:T(8,128)}) %reduce-scatter.4.cloned.1.call-update) | async-done | bytes 163856 | tf_op jit(solution)/shard_map/reduce_scatter | solution.py:394
  (523 shorter events, 144.0 us)
Async XLA Ops:
  7.2 159.5 %all-gather.8.cloned.1.call-start = ((), (), s32[]{:S(2)}) async-start(), calls=%async_computation.11 | async-start | bytes 2703360 | tf_op jit(solution)/shard_map/all_gather | solution.py:55
  11.0 157.7 %copy-start.4 = (bf16[2,256,512]{2,1,0:T(8,128)(2,1)S(1)}, bf16[2,256,512]{2,1,0:T(8,128)(2,1)}, u32[]{:S(2)}) copy-start(bf16[2,256,512]{2,1,0:T(8,128)(2,1)} %param.11) | copy-start | bytes 1572868
  11.1 336.7 %all-gather.12.cloned.1.call-start = ((), (), s32[]{:S(2)}) async-start(), calls=%async_computation.13 | async-start | bytes 4718592 | tf_op jit(solution)/shard_map/all_gather | solution.py:68
  11.8 344.0 %all-gather.10.cloned.1.call-start = ((), (), s32[]{:S(2)}) async-start(), calls=%async_computation.12 | async-start | bytes 4718592 | tf_op jit(solution)/shard_map/all_gather | solution.py:67
  12.7 153.5 %collective-permute-start.7 = (s32[196]{0:T(256)S(1)}, s32[196]{0:T(256)S(1)}, u32[]{:S(2)}, u32[]{:S(2)}) collective-permute-start(s32[196]{0:T(256)S(1)} %bitcast.496), channel_id=1, source_target_pairs={{1,0},{2,1},{3,2},{4,3},{5,4},{6,5},{7,6},{8,7},{9,8},{10,9},{11,1... | collective-permute-start | bytes 2360 | tf_op jit(solution)/shard_map/ppermute | solution.py:32
  14.0 152.2 %collective-permute-start.6 = (s32[196]{0:T(256)S(1)}, s32[196]{0:T(256)S(1)}, u32[]{:S(2)}, u32[]{:S(2)}) collective-permute-start(s32[196]{0:T(256)S(1)} %bitcast.495), channel_id=1, source_target_pairs={{0,1},{1,2},{2,3},{3,4},{4,5},{5,6},{6,7},{7,8},{8,9},{9,10},{10,1... | collective-permute-start | bytes 2360 | tf_op jit(solution)/shard_map/ppermute | solution.py:30
  19.5 146.9 %collective-permute-start.3 = (s32[196]{0:T(256)S(1)}, s32[196]{0:T(256)S(1)}, u32[]{:S(2)}, u32[]{:S(2)}) collective-permute-start(s32[196]{0:T(256)S(1)} %bitcast.494), channel_id=1, source_target_pairs={{1,0},{2,1},{3,2},{4,3},{5,4},{6,5},{7,6},{8,7},{9,8},{10,9},{11,1... | collective-permute-start | bytes 2360 | tf_op jit(solution)/shard_map/ppermute | solution.py:32
  20.8 145.6 %collective-permute-start.2 = (s32[196]{0:T(256)S(1)}, s32[196]{0:T(256)S(1)}, u32[]{:S(2)}, u32[]{:S(2)}) collective-permute-start(s32[196]{0:T(256)S(1)} %bitcast.493), channel_id=1, source_target_pairs={{0,1},{1,2},{2,3},{3,4},{4,5},{5,6},{6,7},{7,8},{8,9},{9,10},{10,1... | collective-permute-start | bytes 2360 | tf_op jit(solution)/shard_map/ppermute | solution.py:30
  26.1 196.0 %copy-start.64 = (s32[256,1]{0,1:T(1,128)}, s32[256,1]{0,1:T(1,128)S(1)}, u32[]{:S(2)}) copy-start(s32[256,1]{0,1:T(1,128)S(1)} %get-tuple-element.144) | copy-start | bytes 3076
  26.1 196.0 %copy-start.67 = (s32[256,1]{0,1:T(1,128)}, s32[256,1]{0,1:T(1,128)S(1)}, u32[]{:S(2)}) copy-start(s32[256,1]{0,1:T(1,128)S(1)} %get-tuple-element.145) | copy-start | bytes 3076
  26.8 237.7 %copy-start.59 = (s32[256,1]{0,1:T(1,128)}, s32[256,1]{0,1:T(1,128)S(1)}, u32[]{:S(2)}) copy-start(s32[256,1]{0,1:T(1,128)S(1)} %get-tuple-element.147) | copy-start | bytes 3076
  28.7 142.1 %copy-start.84 = (f32[256]{0:T(256)}, f32[256]{0:T(256)S(1)}, u32[]{:S(2)}) copy-start(f32[256]{0:T(256)S(1)} %get-tuple-element.180) | copy-start | bytes 3076
  28.7 150.1 %copy-start.77 = (f32[256]{0:T(256)}, f32[256]{0:T(256)S(1)}, u32[]{:S(2)}) copy-start(f32[256]{0:T(256)S(1)} %get-tuple-element.181) | copy-start | bytes 3076
  30.0 140.8 %copy-start.108 = (f32[256]{0:T(256)}, f32[256]{0:T(256)S(1)}, u32[]{:S(2)}) copy-start(f32[256]{0:T(256)S(1)} %get-tuple-element.75) | copy-start | bytes 3076
  30.0 140.8 %copy-start.110 = (f32[256]{0:T(256)}, f32[256]{0:T(256)S(1)}, u32[]{:S(2)}) copy-start(f32[256]{0:T(256)S(1)} %get-tuple-element.74) | copy-start | bytes 3076
  30.0 140.8 %copy-start.104 = (f32[256]{0:T(256)}, f32[256]{0:T(256)S(1)}, u32[]{:S(2)}) copy-start(f32[256]{0:T(256)S(1)} %fusion.165) | copy-start | bytes 3076
  163.3 15.5 %copy-start.88 = (f32[256]{0:T(256)}, f32[256]{0:T(256)S(1)}, u32[]{:S(2)}) copy-start(f32[256]{0:T(256)S(1)} %fusion.163) | copy-start | bytes 3076
  168.5 51.9 %copy-start.70 = (f32[512]{0:T(512)}, f32[512]{0:T(512)S(1)}, u32[]{:S(2)}) copy-start(f32[512]{0:T(512)S(1)} %get-tuple-element.183) | copy-start | bytes 6148
  171.9 20.6 %collective-permute-start.5 = (bf16[2,196,512]{2,1,0:T(8,128)(2,1)}, bf16[2,196,512]{2,1,0:T(8,128)(2,1)}, u32[]{:S(2)}, u32[]{:S(2)}) collective-permute-start(bf16[2,196,512]{2,1,0:T(8,128)(2,1)} %get-tuple-element.117), channel_id=1, source_target_pairs={{1,0},{2,1},{3,2},{4,3},{5,4},{6,5},{7,6},{8,7},{9,8},{10,9},{11,1... | collective-permute-start | bytes 1204232 | tf_op jit(solution)/shard_map/ppermute | solution.py:32
  173.2 19.3 %collective-permute-start.4 = (bf16[2,196,512]{2,1,0:T(8,128)(2,1)}, bf16[2,196,512]{2,1,0:T(8,128)(2,1)}, u32[]{:S(2)}, u32[]{:S(2)}) collective-permute-start(bf16[2,196,512]{2,1,0:T(8,128)(2,1)} %get-tuple-element.116), channel_id=1, source_target_pairs={{0,1},{1,2},{2,3},{3,4},{4,5},{5,6},{6,7},{7,8},{8,9},{9,10},{10,1... | collective-permute-start | bytes 1204232 | tf_op jit(solution)/shard_map/ppermute | solution.py:30
  179.5 13.1 %copy-start.36 = (bf16[3,256,512]{2,1,0:T(8,128)(2,1)}, bf16[3,256,512]{2,1,0:T(8,128)(2,1)S(1)}, u32[]{:S(2)}) copy-start(bf16[3,256,512]{2,1,0:T(8,128)(2,1)S(1)} %fusion.21) | copy-start | bytes 2359300
  179.7 17.9 %copy-start.43 = (bf16[1,256,512]{1,2,0:T(8,128)(2,1)}, bf16[1,256,512]{1,2,0:T(8,128)(2,1)S(1)}, u32[]{:S(2)}) copy-start(bf16[1,256,512]{1,2,0:T(8,128)(2,1)S(1)} %copy.223) | copy-start | bytes 786436
  180.7 28.0 %collective-permute-start.1 = (bf16[2,196,512]{2,1,0:T(8,128)(2,1)}, bf16[2,196,512]{2,1,0:T(8,128)(2,1)}, u32[]{:S(2)}, u32[]{:S(2)}) collective-permute-start(bf16[2,196,512]{2,1,0:T(8,128)(2,1)} %get-tuple-element.115), channel_id=1, source_target_pairs={{1,0},{2,1},{3,2},{4,3},{5,4},{6,5},{7,6},{8,7},{9,8},{10,9},{11,1... | collective-permute-start | bytes 1204232 | tf_op jit(solution)/shard_map/ppermute | solution.py:32
  182.0 26.7 %collective-permute-start = (bf16[2,196,512]{2,1,0:T(8,128)(2,1)}, bf16[2,196,512]{2,1,0:T(8,128)(2,1)}, u32[]{:S(2)}, u32[]{:S(2)}) collective-permute-start(bf16[2,196,512]{2,1,0:T(8,128)(2,1)} %get-tuple-element.114), channel_id=1, source_target_pairs={{0,1},{1,2},{2,3},{3,4},{4,5},{5,6},{6,7},{7,8},{8,9},{9,10},{10,1... | collective-permute-start | bytes 1204232 | tf_op jit(solution)/shard_map/ppermute | solution.py:30
  200.1 15.9 %copy-start.53 = (bf16[8,64,256]{2,1,0:T(8,128)(2,1)}, bf16[8,64,256]{2,1,0:T(8,128)(2,1)S(1)}, u32[]{:S(2)}) copy-start(bf16[8,64,256]{2,1,0:T(8,128)(2,1)S(1)} %convolution_convert_fusion.8) | copy-start | bytes 786436
  200.1 14.8 %copy-start.41 = (bf16[1,256,512]{1,2,0:T(8,128)(2,1)S(1)}, bf16[1,256,512]{1,2,0:T(8,128)(2,1)}, u32[]{:S(2)}) copy-start(bf16[1,256,512]{1,2,0:T(8,128)(2,1)} %copy.214) | copy-start | bytes 786436
  201.7 328.3 %copy-start.75 = (f32[256]{0:T(256)}, f32[256]{0:T(256)S(1)}, u32[]{:S(2)}) copy-start(f32[256]{0:T(256)S(1)} %broadcast_multiply_fusion) | copy-start | bytes 3076
  201.9 14.1 %copy-start.112 = (f32[256]{0:T(256)}, f32[256]{0:T(256)S(1)}, u32[]{:S(2)}) copy-start(f32[256]{0:T(256)S(1)} %multiply_reduce_fusion.12) | copy-start | bytes 3076
  201.9 18.4 %copy-start.90 = (f32[256]{0:T(256)}, f32[256]{0:T(256)S(1)}, u32[]{:S(2)}) copy-start(f32[256]{0:T(256)S(1)} %fusion.166) | copy-start | bytes 3076
  220.1 310.0 %copy-start.76 = (f32[256]{0:T(256)}, f32[256]{0:T(256)S(1)}, u32[]{:S(2)}) copy-start(f32[256]{0:T(256)S(1)} %broadcast_multiply_fusion.2) | copy-start | bytes 3076
  220.9 69.5 %copy-start.31 = (bf16[256,512]{1,0:T(8,128)(2,1)}, bf16[256,512]{1,0:T(8,128)(2,1)S(1)}, u32[]{:S(2)}) copy-start(bf16[256,512]{1,0:T(8,128)(2,1)S(1)} %get-tuple-element.129) | copy-start | bytes 786436
  222.1 304.2 %copy-start.62 = (f32[256]{0:T(256)}, f32[256]{0:T(256)S(1)}, u32[]{:S(2)}) copy-start(f32[256]{0:T(256)S(1)} %get-tuple-element.170) | copy-start | bytes 3076
  222.2 16.1 %copy-start.82 = (f32[256]{0:T(256)}, f32[256]{0:T(256)S(1)}, u32[]{:S(2)}) copy-start(f32[256]{0:T(256)S(1)} %fusion.129) | copy-start | bytes 3076
  226.4 34.8 %copy-start.23 = (f32[256,512]{1,0:T(8,128)S(1)}, f32[256,512]{1,0:T(8,128)}, u32[]{:S(2)}) copy-start(f32[256,512]{1,0:T(8,128)} %get-tuple-element.121) | copy-start | bytes 1572868
  227.5 29.2 %all-to-all-start.4 = ((bf16[8,1,128,512]{3,2,1,0:T(8,128)(2,1)}), bf16[8,1,128,512]{3,2,1,0:T(8,128)(2,1)}, u32[]{:S(2)}, u32[]{:S(2)}) async-start(bf16[8,1,128,512]{3,2,1,0:T(8,128)(2,1)} %bitcast.390), calls=%async_computation.4 | async-start | bytes 2097152 | tf_op jit(solution)/shard_map/all_to_all | solution.py:243
  256.6 29.5 %all-to-all-start = ((bf16[8,1,128,512]{3,2,1,0:T(8,128)(2,1)}), bf16[8,1,128,512]{3,2,1,0:T(8,128)(2,1)}, u32[]{:S(2)}, u32[]{:S(2)}) async-start(bf16[8,1,128,512]{3,2,1,0:T(8,128)(2,1)} %bitcast.389), calls=%async_computation | async-start | bytes 2097152 | tf_op jit(solution)/shard_map/all_to_all | solution.py:175
  264.5 31.5 %copy-start.79 = (f32[256]{0:T(256)}, f32[256]{0:T(256)S(1)}, u32[]{:S(2)}) copy-start(f32[256]{0:T(256)S(1)} %fusion.131) | copy-start | bytes 3076
  286.2 29.5 %all-to-all-start.6 = ((bf16[8,1,128,512]{3,2,1,0:T(8,128)(2,1)}), bf16[8,1,128,512]{3,2,1,0:T(8,128)(2,1)}, u32[]{:S(2)}, u32[]{:S(2)}) async-start(bf16[8,1,128,512]{3,2,1,0:T(8,128)(2,1)} %bitcast.391), calls=%async_computation.6 | async-start | bytes 2097152 | tf_op jit(solution)/shard_map/all_to_all | solution.py:243
  315.7 29.7 %all-to-all-start.2 = ((bf16[8,1,128,512]{3,2,1,0:T(8,128)(2,1)}), bf16[8,1,128,512]{3,2,1,0:T(8,128)(2,1)}, u32[]{:S(2)}, u32[]{:S(2)}) async-start(bf16[8,1,128,512]{3,2,1,0:T(8,128)(2,1)} %bitcast.392), calls=%async_computation.2 | async-start | bytes 2097152 | tf_op jit(solution)/shard_map/all_to_all | solution.py:175
  377.5 37.1 %all-to-all-start.5 = ((bf16[2,4,128,512]{3,2,0,1:T(8,128)(2,1)}), bf16[2,4,128,512]{3,2,0,1:T(8,128)(2,1)S(1)}, u32[]{:S(2)}, u32[]{:S(2)}) async-start(bf16[2,4,128,512]{3,2,0,1:T(8,128)(2,1)} %copy.234), calls=%async_computation.5 | async-start | bytes 2097152 | tf_op jit(solution)/shard_map/all_to_all | solution.py:265
  381.0 257.7 %reduce-scatter.6.cloned.1.call-start = ((), (), s32[]{:S(2)}) async-start(), calls=%async_computation.15 | async-start | bytes 4718592 | tf_op jit(solution)/shard_map/reduce_scatter | solution.py:403
  381.0 18.1 %slice-start.4 = ((s8[8388608]{0:T(1024)(128)(4,1)}), s8[4194304]{0:T(1024)(128)(4,1)S(1)}, s32[]{:S(2)}) async-start(s8[8388608]{0:T(1024)(128)(4,1)} %bitcast.371), calls=%async_computation.21 | async-start | bytes 8388608
  386.1 13.0 %slice-start.5 = ((s8[8388608]{0:T(1024)(128)(4,1)}), s8[4194304]{0:T(1024)(128)(4,1)S(1)}, s32[]{:S(2)}) async-start(s8[8388608]{0:T(1024)(128)(4,1)} %bitcast.371), calls=%async_computation.22 | async-start | bytes 8388608
  414.6 29.8 %all-to-all-start.1 = ((bf16[2,4,128,512]{3,2,0,1:T(8,128)(2,1)}), bf16[2,4,128,512]{3,2,0,1:T(8,128)(2,1)}, u32[]{:S(2)}, u32[]{:S(2)}) async-start(bf16[2,4,128,512]{3,2,0,1:T(8,128)(2,1)} %copy.220), calls=%async_computation.1 | async-start | bytes 2097152 | tf_op jit(solution)/shard_map/all_to_all | solution.py:185
  444.3 29.1 %all-to-all-start.7 = ((bf16[2,4,128,512]{3,2,0,1:T(8,128)(2,1)}), bf16[2,4,128,512]{3,2,0,1:T(8,128)(2,1)S(1)}, u32[]{:S(2)}, u32[]{:S(2)}) async-start(bf16[2,4,128,512]{3,2,0,1:T(8,128)(2,1)} %copy.243), calls=%async_computation.7 | async-start | bytes 2097152 | tf_op jit(solution)/shard_map/all_to_all | solution.py:265
  473.4 13.6 %copy-start.29 = (bf16[2,4,128,512]{3,2,0,1:T(8,128)(2,1)}, bf16[2,4,128,512]{3,2,0,1:T(8,128)(2,1)S(1)}, u32[]{:S(2)}) copy-start(bf16[2,4,128,512]{3,2,0,1:T(8,128)(2,1)S(1)} %all-to-all-done.7) | copy-start | bytes 3145732
  473.4 38.6 %all-to-all-start.3 = ((bf16[2,4,128,512]{3,2,0,1:T(8,128)(2,1)}), bf16[2,4,128,512]{3,2,0,1:T(8,128)(2,1)}, u32[]{:S(2)}, u32[]{:S(2)}) async-start(bf16[2,4,128,512]{3,2,0,1:T(8,128)(2,1)} %copy.229), calls=%async_computation.3 | async-start | bytes 2097152 | tf_op jit(solution)/shard_map/all_to_all | solution.py:185
  477.7 163.1 %reduce-scatter.8.cloned.1.call-start = ((), (), s32[]{:S(2)}) async-start(), calls=%async_computation.16 | async-start | bytes 4718592 | tf_op jit(solution)/shard_map/reduce_scatter | solution.py:406
  487.0 351.3 %reduce-scatter.4.cloned.1.call-start = ((), (), s32[]{:S(2)}) async-start(), calls=%async_computation.14 | async-start | bytes 8650752 | tf_op jit(solution)/shard_map/reduce_scatter | solution.py:394
  516.1 13.9 %copy-start.60 = (s32[256,1]{0,1:T(1,128)S(1)}, s32[256,1]{0,1:T(1,128)}, u32[]{:S(2)}) copy-start(s32[256,1]{0,1:T(1,128)} %copy-done.59) | copy-start | bytes 3076
  516.1 13.9 %copy-start.80 = (f32[256]{0:T(256)S(1)}, f32[256]{0:T(256)}, u32[]{:S(2)}) copy-start(f32[256]{0:T(256)} %copy-done.79) | copy-start | bytes 3076
  516.1 14.0 %copy-start.71 = (f32[512]{0:T(512)S(1)}, f32[512]{0:T(512)}, u32[]{:S(2)}) copy-start(f32[512]{0:T(512)} %copy-done.70) | copy-start | bytes 6148
  518.8 13.6 %copy-start.113 = (f32[256]{0:T(256)S(1)}, f32[256]{0:T(256)}, u32[]{:S(2)}) copy-start(f32[256]{0:T(256)} %copy-done.112) | copy-start | bytes 3076
  518.8 13.7 %copy-start.115 = (f32[256]{0:T(256)S(1)}, f32[256]{0:T(256)}, u32[]{:S(2)}) copy-start(f32[256]{0:T(256)} %copy-done.114) | copy-start | bytes 3076
  518.8 13.7 %copy-start.45 = (f32[256,512]{1,0:T(8,128)S(1)}, f32[256,512]{1,0:T(8,128)}, u32[]{:S(2)}) copy-start(f32[256,512]{1,0:T(8,128)} %get-tuple-element.63) | copy-start | bytes 1572868
  518.8 13.7 %copy-start.72 = (f32[512]{0:T(512)S(1)}, f32[512]{0:T(512)}, u32[]{:S(2)}) copy-start(f32[512]{0:T(512)} %copy-done.70) | copy-start | bytes 6148
  547.4 14.0 %copy-start.100 = (f32[256]{0:T(256)}, f32[256]{0:T(256)S(1)}, u32[]{:S(2)}) copy-start(f32[256]{0:T(256)S(1)} %negate_multiply_fusion.3) | copy-start | bytes 3076
  568.2 15.3 %copy-start.73 = (f32[8,256]{1,0:T(8,128)S(1)}, f32[8,256]{1,0:T(8,128)}, u32[]{:S(2)}) copy-start(f32[8,256]{1,0:T(8,128)} %get-tuple-element.177) | copy-start | bytes 24580
  574.1 37.7 %collective-permute-start.11 = (bf16[2,196,512]{2,1,0:T(8,128)(2,1)}, bf16[2,196,512]{2,1,0:T(8,128)(2,1)}, u32[]{:S(2)}, u32[]{:S(2)}) collective-permute-start(bf16[2,196,512]{2,1,0:T(8,128)(2,1)} %get-tuple-element.105), channel_id=1, source_target_pairs={{1,0},{2,1},{3,2},{4,3},{5,4},{6,5},{7,6},{8,7},{9,8},{10,9},{11,1... | collective-permute-start | bytes 1204232 | tf_op jit(solution)/shard_map/ppermute | solution.py:32
  575.3 36.4 %collective-permute-start.10 = (bf16[2,196,512]{2,1,0:T(8,128)(2,1)}, bf16[2,196,512]{2,1,0:T(8,128)(2,1)}, u32[]{:S(2)}, u32[]{:S(2)}) collective-permute-start(bf16[2,196,512]{2,1,0:T(8,128)(2,1)} %get-tuple-element.104), channel_id=1, source_target_pairs={{0,1},{1,2},{2,3},{3,4},{4,5},{5,6},{6,7},{7,8},{8,9},{9,10},{10,1... | collective-permute-start | bytes 1204232 | tf_op jit(solution)/shard_map/ppermute | solution.py:30
  592.7 13.0 %copy-start.83 = (f32[256]{0:T(256)S(1)}, f32[256]{0:T(256)}, u32[]{:S(2)}) copy-start(f32[256]{0:T(256)} %copy-done.82) | copy-start | bytes 3076
  592.8 13.2 %copy-start.101 = (f32[256]{0:T(256)S(1)}, f32[256]{0:T(256)}, u32[]{:S(2)}) copy-start(f32[256]{0:T(256)} %copy-done.100) | copy-start | bytes 3076
  598.9 14.7 %collective-permute-start.9 = (bf16[2,196,512]{2,1,0:T(8,128)(2,1)}, bf16[2,196,512]{2,1,0:T(8,128)(2,1)}, u32[]{:S(2)}, u32[]{:S(2)}) collective-permute-start(bf16[2,196,512]{2,1,0:T(8,128)(2,1)} %get-tuple-element.107), channel_id=1, source_target_pairs={{1,0},{2,1},{3,2},{4,3},{5,4},{6,5},{7,6},{8,7},{9,8},{10,9},{11,1... | collective-permute-start | bytes 1204232 | tf_op jit(solution)/shard_map/ppermute | solution.py:32
  600.4 14.7 %collective-permute-start.8 = (bf16[2,196,512]{2,1,0:T(8,128)(2,1)}, bf16[2,196,512]{2,1,0:T(8,128)(2,1)}, u32[]{:S(2)}, u32[]{:S(2)}) collective-permute-start(bf16[2,196,512]{2,1,0:T(8,128)(2,1)} %get-tuple-element.106), channel_id=1, source_target_pairs={{0,1},{1,2},{2,3},{3,4},{4,5},{5,6},{6,7},{7,8},{8,9},{9,10},{10,1... | collective-permute-start | bytes 1204232 | tf_op jit(solution)/shard_map/ppermute | solution.py:30
  (95 other events, 592.5 us)
Sparse Core Ops, SparseCore 0:
  11.6 60.5 all-gather.7
  74.1 35.6 all-gather.11
  111.8 36.7 all-gather.9
  403.6 61.3 reduce-scatter.5
  487.1 61.3 reduce-scatter.7
  634.7 203.5 reduce-scatter.3
